TPU v7x, 32 devices: a whole 2x2x4 slice. The times are simulated.
32 devices in a mesh: sec: 4 (over x, core), key: 8 (over z, y).
Axes of the slice: x: 2, y: 2, z: 4, core: 2. Of those that a mesh axis runs over, the one named last changes fastest.
Arguments:
- query: bfloat16 [4096, 16, 128], P(('sec', 'key')), may hold values from -64 to 64
- key: bfloat16 [4096, 4, 128], P(('sec', 'key')), may hold values from -5 to 5
- value: bfloat16 [4096, 4, 128], P(('sec', 'key')), may hold values from -5 to 5
- raw_directions: bfloat16 [4096, 4, 128], P(('sec', 'key')), may hold values from -5 to 5
- beta_raw_logits: float32 [4096, 4], P(('sec', 'key')), may hold values from -7 to 7
Outputs:
- attended: bfloat16 [4096, 16, 128], P(('sec', 'key'))
All inputs are finite; a program needn't handle non-finite values.
Results may differ from a plain program's by a relative error of at most 0.0055.
Values sent between devices are 32-bit elements; how exact they have to be, the bound alone decides.
No kernel may reach another device: no remote copies, remote signals or barrier semaphores. Data moves between devices by JAX's collectives and lax.ppermute only.
A program may use at most 64 MiB of HBM per device.

v0:
```python
import math

import jax
import jax.numpy as jnp
from jax import lax
from jax.sharding import PartitionSpec as P

highest = lax.Precision.HIGHEST


def carried_in(value, axis, join, neutral, backward):
    count, mine = (lax.axis_size(axis), lax.axis_index(axis))
    pieces = lax.all_gather(value, axis)
    if backward:
        pieces = pieces[::-1]
        mine = count - 1 - mine
    total = jnp.full_like(value, 0) + jnp.asarray(neutral, value.dtype)

    def turn(position, total):
        longer = join(total, pieces[position])
        return jnp.where(position < mine, longer, total)

    return lax.fori_loop(0, count - 1, turn, total)


def shifted(value, axis, steps):
    count = lax.axis_size(axis)
    first, last = (max(0, -steps), min(count, count - steps))
    return lax.ppermute(value, axis, [(source, source + steps) for source in range(first, last)])


def block_terms(query, key, raw_directions, beta_raw_logits):
    length = key.shape[0]
    heads = key.shape[1]
    width = key.shape[2]
    query_group = query.shape[1] // heads
    w_float = raw_directions.astype(jnp.float32)
    w_unit = w_float / jnp.sqrt(jnp.sum(w_float * w_float, -1, keepdims=True) + 1e-06)
    beta = 2.0 * jax.nn.sigmoid(beta_raw_logits)
    w_heads = jnp.transpose(w_unit, (1, 0, 2))
    k_heads = jnp.transpose(key.astype(jnp.float32), (1, 0, 2))
    b_heads = jnp.transpose(beta, (1, 0))[:, :, None]
    positions = jnp.arange(length)
    strict = (positions[:, None] > positions[None, :]).astype(jnp.float32)
    lower = (positions[:, None] >= positions[None, :]).astype(jnp.float32)
    gram = jnp.einsum("hte,hse->hts", w_heads, w_heads, precision=highest) * strict
    system = jnp.eye(length, dtype=jnp.float32) + b_heads * gram
    cross = jnp.einsum("hte,hse->hts", w_heads, k_heads, precision=highest) * strict
    right = jnp.concatenate([b_heads * w_heads, b_heads * cross], axis=2)
    solved = lax.linalg.triangular_solve(
        system, right, left_side=True, lower=True, unit_diagonal=True
    )
    y_rows = solved[:, :, :width]
    z_rows = solved[:, :, width:]
    block_map = jnp.eye(width, dtype=jnp.float32) - jnp.einsum(
        "hte,htf->hef", w_heads, y_rows, precision=highest
    )
    key_end = k_heads - jnp.einsum("hts,hte->hse", z_rows, w_heads, precision=highest)
    q_heads = jnp.transpose(
        query.astype(jnp.float32).reshape(length, heads, query_group, width), (1, 2, 0, 3)
    )
    q_dot_w = jnp.einsum("hgie,hte->hgit", q_heads, w_heads, precision=highest) * lower
    query_start = q_heads - jnp.einsum("hgit,hte->hgie", q_dot_w, y_rows, precision=highest)
    inner = jnp.einsum("hgie,hje->hgij", q_heads, k_heads, precision=highest)
    inner = inner - jnp.einsum("hgit,htj->hgij", q_dot_w, z_rows, precision=highest)
    query_start = query_start.reshape(heads, query_group * length, width)
    inner = inner.reshape(heads, query_group * length, length) * width ** (-0.5)
    return (query_start, key_end, block_map, inner)


def attend(state, scores, values, valid):
    score_maxima, weighted_totals, exponent_sums = state
    masked = jnp.where(valid, scores, -1e30)
    new_max = jnp.maximum(score_maxima, jnp.max(masked, -1))
    weights = jnp.where(valid, jnp.exp(masked - new_max[..., None]), 0.0)
    factor = jnp.exp(score_maxima - new_max)
    weighted_totals = weighted_totals * factor + jnp.sum(weights, -1)
    rounded = weights.astype(jnp.bfloat16)
    exponent_sums = exponent_sums * factor[..., None] + jnp.einsum(
        "...ij,...je->...ie", rounded, values, preferred_element_type=jnp.float32
    )
    return (new_max, weighted_totals, exponent_sums)


def attend_packet(state, queries_flat, packet, valid, width):
    count = packet.shape[0]
    block = math.gcd(count, 512)
    scale_factor = width ** (-0.5)

    def one_block(index, carry):
        piece = lax.dynamic_slice_in_dim(packet, index * block, block, 0)
        scores = (
            jnp.einsum("ie,je->ij", queries_flat, piece[:, :width], precision=highest)
            * scale_factor
        )
        return attend(carry, scores, piece[:, width:].astype(jnp.bfloat16), valid)

    return lax.fori_loop(0, count // block, one_block, state)


def later_first(earlier, later):
    return jnp.einsum("hij,hjk->hik", later, earlier, precision=highest)


def earlier_first(earlier, later):
    return jnp.einsum("hij,hjk->hik", earlier, later, precision=highest)


def body(query, key, value, raw_directions, beta_raw_logits):
    length = query.shape[0]
    q_count = query.shape[1]
    width = query.shape[2]
    kv_heads = key.shape[1]
    query_group = q_count // kv_heads
    key_count = lax.axis_size("key")
    sec_count = lax.axis_size("sec")
    key_index = lax.axis_index("key")
    sec_index = lax.axis_index("sec")
    per_slot = q_count // key_count
    repeat_count = key_count // kv_heads
    rows_section = length * key_count
    scale_factor = width ** (-0.5)
    query_start, key_end, block_map, inner = block_terms(
        query, key, raw_directions, beta_raw_logits
    )
    value_head_rows = jnp.transpose(value, (1, 0, 2))
    positions = jnp.arange(length)
    causal = jnp.tile(positions[:, None] >= positions[None, :], (query_group, 1))
    local = (
        jnp.full((kv_heads, query_group * length), -1e30, jnp.float32),
        jnp.zeros((kv_heads, query_group * length), jnp.float32),
        jnp.zeros((kv_heads, query_group * length, width), jnp.float32),
    )
    local = attend(local, inner, value_head_rows, causal)
    packed = jnp.concatenate([key_end, value_head_rows.astype(jnp.float32)], axis=2)
    gathered_pack, gathered_maps = (
        lax.all_gather(packed, "key", axis=1, tiled=True),
        lax.all_gather(block_map, "key", axis=0, tiled=True),
    )
    gathered_maps = gathered_maps.reshape(key_count, kv_heads, width, width)

    def replay_step(step, carry):
        moving = carry[0]
        source = jnp.maximum(key_index - step, 0)
        piece = lax.dynamic_slice_in_dim(gathered_pack, source * length, length, 1)
        scores = (
            jnp.einsum("hie,hje->hij", moving, piece[:, :, :width], precision=highest)
            * scale_factor
        )
        state = attend(
            carry[1:], scores, piece[:, :, width:].astype(jnp.bfloat16), key_index - step >= 0
        )
        source_map = lax.dynamic_index_in_dim(gathered_maps, source, 0, keepdims=False)
        moving = jnp.einsum("hie,hef->hif", moving, source_map, precision=highest)
        return (moving,) + state

    local = lax.fori_loop(1, key_count, replay_step, (query_start,) + local)[1:]
    eye_maps = jnp.broadcast_to(jnp.eye(width, dtype=jnp.float32), block_map.shape)
    before = carried_in(block_map, "key", later_first, eye_maps, False)
    after = carried_in(block_map, "key", earlier_first, eye_maps, True)
    section_map = jnp.einsum(
        "hij,hjk->hik",
        after,
        jnp.einsum("hij,hjk->hik", block_map, before, precision=highest),
        precision=highest,
    )
    query_section = jnp.einsum("hie,hef->hif", query_start, before, precision=highest)
    query_section = jnp.transpose(
        query_section.reshape(kv_heads, query_group, length, width), (2, 0, 1, 3)
    )
    key_section = jnp.einsum("hje,hfe->hjf", key_end, after, precision=highest)
    key_pack = jnp.concatenate(
        [jnp.transpose(key_section, (1, 0, 2)), value.astype(jnp.float32)], axis=2
    )
    own_map = lax.dynamic_index_in_dim(section_map, key_index // repeat_count, 0, keepdims=False)
    query_slots = query_section.reshape(length, key_count, per_slot, width)
    key_slots = jnp.repeat(key_pack, repeat_count, axis=1)
    slot_queries, slot_keys = (
        lax.all_to_all(query_slots, "key", split_axis=1, concat_axis=0, tiled=True),
        lax.all_to_all(key_slots, "key", split_axis=1, concat_axis=0, tiled=True),
    )
    slot_flat = jnp.transpose(
        slot_queries.reshape(rows_section, per_slot, width), (1, 0, 2)
    ).reshape(per_slot * rows_section, width)
    slot_keys = slot_keys.reshape(rows_section, 2 * width)
    flat_rows = slot_flat.shape[0]
    distant = (
        jnp.full((flat_rows,), -1e30, jnp.float32),
        jnp.zeros((flat_rows,), jnp.float32),
        jnp.zeros((flat_rows, width), jnp.float32),
    )

    def walk_step(step, carry):
        arrived = shifted(carry[0], "sec", 1)
        state = attend_packet(carry[1:], slot_flat, arrived, sec_index - step >= 0, width)
        moved = jnp.einsum("je,fe->jf", arrived[:, :width], own_map, precision=highest)
        return (jnp.concatenate([moved, arrived[:, width:]], axis=1),) + state

    distant = lax.fori_loop(1, sec_count, walk_step, (slot_keys,) + distant)[1:]
    far_max = jnp.transpose(distant[0].reshape(per_slot, rows_section), (1, 0))
    far_total = jnp.transpose(distant[1].reshape(per_slot, rows_section), (1, 0))
    far_sums = jnp.transpose(distant[2].reshape(per_slot, rows_section, width), (1, 0, 2))
    back_sums, back_max, back_total = (
        lax.all_to_all(far_sums, "key", split_axis=0, concat_axis=1, tiled=True),
        lax.all_to_all(far_max, "key", split_axis=0, concat_axis=1, tiled=True),
        lax.all_to_all(far_total, "key", split_axis=0, concat_axis=1, tiled=True),
    )
    near_max = jnp.transpose(local[0].reshape(kv_heads, query_group, length), (2, 0, 1)).reshape(
        length, q_count
    )
    near_total = jnp.transpose(local[1].reshape(kv_heads, query_group, length), (2, 0, 1)).reshape(
        length, q_count
    )
    near_sums = jnp.transpose(
        local[2].reshape(kv_heads, query_group, length, width), (2, 0, 1, 3)
    ).reshape(length, q_count, width)
    joint_max = jnp.maximum(near_max, back_max)
    near_factor = jnp.exp(near_max - joint_max)
    far_factor = jnp.exp(back_max - joint_max)
    weighted_totals = near_total * near_factor + back_total * far_factor
    exponent_sums = near_sums * near_factor[..., None] + back_sums * far_factor[..., None]
    return (exponent_sums / weighted_totals[..., None]).astype(jnp.bfloat16)


def solution(mesh):
    return jax.shard_map(
        body,
        mesh=mesh,
        in_specs=(
            P(("sec", "key"), None, None),
            P(("sec", "key"), None, None),
            P(("sec", "key"), None, None),
            P(("sec", "key"), None, None),
            P(("sec", "key"), None),
        ),
        out_specs=P(("sec", "key"), None, None),
        check_vma=False,
    )
```

profile of v0, /device:TPU:6, one launch (start us, length us, event | category | flops | bytes accessed | tf_op | source)
XLA Modules:
  0.0 414.8 jit_solution(6768845351763684802)
XLA Ops:
  11.4 39.3 %custom-call.3 = f32[4,1,128,128]{2,3,1,0:T(8,128)S(1)} custom-call(f32[4,1,128,128]{3,2,1,0:T(8,128)S(1)} %fusion.41), custom_call_target="InvertDiagBlocksLowerTriangular" | custom-call | tf_op jit(solution)/shard_map/triangular_solve | solution.py:50
  60.5 44.1 %all-gather.4.cloned.1.call-done = f32[32,128,128]{2,1,0:T(8,128)} async-done(((f32[4,128,128]{2,1,0:T(8,128)}), f32[32,128,128]{2,1,0:T(8,128)}) %all-gather.4.cloned.1.call-update) | async-done | bytes 2097168 | tf_op jit(solution)/shard_map/all_gather | solution.py:138
  107.8 9.8 %while.97 = (s32[]{:T(128)}, f32[4,128,128]{2,1,0:T(8,128)S(1)}, s32[]{:T(128)}, f32[8,4,128,128]{3,2,1,0:T(8,128)}, s32[]{:T(128)}) while((s32[]{:T(128)}, f32[4,128,128]{2,1,0:T(8,128)S(1)}, s32[]{:T(128)}, f32[8,4,128,128]{3,2,1,0:T(8,128)}, s32[]{:T(128)}) %tuple.182), condition=%wide.region_10.11_spmd, body=%wide.region_9.10_spmd.sunk | while | flops 100728832 | bytes 1573447 | solution.py:23
  119.6 4.9 %all-to-all-start.1 = ((f32[128,8,2,128]{3,0,2,1:T(8,128)}), f32[128,8,2,128]{3,0,2,1:T(8,128)S(1)}, u32[]{:S(2)}, u32[]{:S(2)}) async-start(f32[128,8,2,128]{3,0,2,1:T(8,128)} %bitcast.46), calls=%async_computation.1 | async-start | bytes 2097152 | tf_op jit(solution)/shard_map/all_to_all | solution.py:179
  124.6 11.2 %while.96 = (s32[]{:T(128)}, f32[4,128,128]{1,2,0:T(8,128)S(1)}, s32[]{:T(128)}, f32[8,4,128,128]{3,2,1,0:T(8,128)}, s32[]{:T(128)}) while((s32[]{:T(128)}, f32[4,128,128]{1,2,0:T(8,128)S(1)}, s32[]{:T(128)}, f32[8,4,128,128]{3,2,1,0:T(8,128)}, s32[]{:T(128)}) %tuple.165), condition=%wide.region_8.9_spmd, body=%wide.region_7.8_spmd.sunk | while | flops 100728832 | bytes 1573447 | solution.py:23
  136.5 12.3 %all-to-all-done.1 = f32[128,8,2,128]{3,0,2,1:T(8,128)S(1)} async-done(((f32[128,8,2,128]{3,0,2,1:T(8,128)}), f32[128,8,2,128]{3,0,2,1:T(8,128)S(1)}, u32[]{:S(2)}, u32[]{:S(2)}) %all-to-all-start.1) | async-done | bytes 1048608 | tf_op jit(solution)/shard_map/all_to_all | solution.py:179
  149.9 4.3 %all-to-all-start = ((f32[128,8,256]{0,2,1:T(8,128)}), f32[128,8,256]{0,2,1:T(8,128)S(1)}, u32[]{:S(2)}, u32[]{:S(2)}) async-start(f32[128,8,256]{0,2,1:T(8,128)} %bitcast.228), calls=%async_computation | async-start | bytes 2097152 | tf_op jit(solution)/shard_map/all_to_all | solution.py:180
  157.3 36.5 %all-to-all-done = f32[128,8,256]{0,2,1:T(8,128)S(1)} async-done(((f32[128,8,256]{0,2,1:T(8,128)}), f32[128,8,256]{0,2,1:T(8,128)S(1)}, u32[]{:S(2)}, u32[]{:S(2)}) %all-to-all-start) | async-done | bytes 1048608 | tf_op jit(solution)/shard_map/all_to_all | solution.py:180
  195.5 122.5 %while.99 = (s32[]{:T(128)}, f32[1024,256]{0,1:T(8,128)S(1)}, f32[2048]{0:T(1024)S(1)}, f32[2048]{0:T(1024)S(1)}, f32[2048,128]{1,0:T(8,128)}, /*index=5*/f32[12...) while((s32[]{:T(128)}, f32[1024,256]{0,1:T(8,128)S(1)}, ...), condition=%wide.region_16.17_spmd, body=%wide.region_11.16_spmd.sunk | while | flops 2094796800 | bytes 44106204 | solution.py:199
  197.4 14.2 %collective-permute-done = f32[1024,256]{0,1:T(8,128)S(1)} collective-permute-done((f32[1024,256]{0,1:T(8,128)S(1)}, f32[1024,256]{0,1:T(8,128)S(1)}, u32[]{:S(2)}, u32[]{:S(2)}) %collective-permute-start) | collective-permute-done | bytes 1048608 | tf_op jit(solution)/shard_map/while/body/eval_jaxpr/ppermute | solution.py:29
  211.6 24.0 %while.100 = (s32[]{:T(128)}, f32[2048]{0:T(1024)S(1)}, f32[2048]{0:T(1024)S(1)}, f32[2048,128]{1,0:T(8,128)}, pred[]{:T(512)}, /*index=5*/f32[1024,256]{0,1:T(8...) while((s32[]{:T(128)}, f32[2048]{0:T(1024)S(1)}, ...), condition=%wide.region_15.15_spmd, body=%wide.region_12.14_spmd.sunk | while | flops 1893208064 | bytes 35651772 | solution.py:98
  218.8 4.9 %convolution_add_fusion.6 = f32[2048,128]{1,0:T(8,128)} fusion(f32[512,2048]{1,0:T(8,128)} %copy-done, f32[2048]{0:T(1024)S(1)} %max.48, pred[]{:T(512)} %get-tuple-element.1047, f32[2048,128]{1,0:T(8,128)} %get-tuple-element.1035, f32[2048]{0:T(1024)S(1)} %get-tuple-element.1020, bf16[512,128]{1,0:T(8,128)(2,1)S(1)} %copy.255), kind=kOutput, calls=%fused_computation.33.clone.1 | convolution fusion | flops 274202624 | bytes 6438913 | tf_op jit(solution)/shard_map/while/body/eval_jaxpr/while/body/eval_jaxpr/...ij,...je->...ie/dot_general | solution.py:79
  230.8 4.9 %convolution_add_fusion.6 = f32[2048,128]{1,0:T(8,128)} fusion(f32[512,2048]{1,0:T(8,128)} %copy-done, f32[2048]{0:T(1024)S(1)} %max.48, pred[]{:T(512)} %get-tuple-element.1047, f32[2048,128]{1,0:T(8,128)} %get-tuple-element.1035, f32[2048]{0:T(1024)S(1)} %get-tuple-element.1020, bf16[512,128]{1,0:T(8,128)(2,1)S(1)} %copy.255), kind=kOutput, calls=%fused_computation.33.clone.1 | convolution fusion | flops 274202624 | bytes 6438913 | tf_op jit(solution)/shard_map/while/body/eval_jaxpr/while/body/eval_jaxpr/...ij,...je->...ie/dot_general | solution.py:79
  238.3 14.2 %collective-permute-done = f32[1024,256]{0,1:T(8,128)S(1)} collective-permute-done((f32[1024,256]{0,1:T(8,128)S(1)}, f32[1024,256]{0,1:T(8,128)S(1)}, u32[]{:S(2)}, u32[]{:S(2)}) %collective-permute-start) | collective-permute-done | bytes 1048608 | tf_op jit(solution)/shard_map/while/body/eval_jaxpr/ppermute | solution.py:29
  252.5 24.0 %while.100 = (s32[]{:T(128)}, f32[2048]{0:T(1024)S(1)}, f32[2048]{0:T(1024)S(1)}, f32[2048,128]{1,0:T(8,128)}, pred[]{:T(512)}, /*index=5*/f32[1024,256]{0,1:T(8...) while((s32[]{:T(128)}, f32[2048]{0:T(1024)S(1)}, ...), condition=%wide.region_15.15_spmd, body=%wide.region_12.14_spmd.sunk | while | flops 1893208064 | bytes 35651772 | solution.py:98
  259.7 4.8 %convolution_add_fusion.6 = f32[2048,128]{1,0:T(8,128)} fusion(f32[512,2048]{1,0:T(8,128)} %copy-done, f32[2048]{0:T(1024)S(1)} %max.48, pred[]{:T(512)} %get-tuple-element.1047, f32[2048,128]{1,0:T(8,128)} %get-tuple-element.1035, f32[2048]{0:T(1024)S(1)} %get-tuple-element.1020, bf16[512,128]{1,0:T(8,128)(2,1)S(1)} %copy.255), kind=kOutput, calls=%fused_computation.33.clone.1 | convolution fusion | flops 274202624 | bytes 6438913 | tf_op jit(solution)/shard_map/while/body/eval_jaxpr/while/body/eval_jaxpr/...ij,...je->...ie/dot_general | solution.py:79
  271.6 4.8 %convolution_add_fusion.6 = f32[2048,128]{1,0:T(8,128)} fusion(f32[512,2048]{1,0:T(8,128)} %copy-done, f32[2048]{0:T(1024)S(1)} %max.48, pred[]{:T(512)} %get-tuple-element.1047, f32[2048,128]{1,0:T(8,128)} %get-tuple-element.1035, f32[2048]{0:T(1024)S(1)} %get-tuple-element.1020, bf16[512,128]{1,0:T(8,128)(2,1)S(1)} %copy.255), kind=kOutput, calls=%fused_computation.33.clone.1 | convolution fusion | flops 274202624 | bytes 6438913 | tf_op jit(solution)/shard_map/while/body/eval_jaxpr/while/body/eval_jaxpr/...ij,...je->...ie/dot_general | solution.py:79
  279.2 14.2 %collective-permute-done = f32[1024,256]{0,1:T(8,128)S(1)} collective-permute-done((f32[1024,256]{0,1:T(8,128)S(1)}, f32[1024,256]{0,1:T(8,128)S(1)}, u32[]{:S(2)}, u32[]{:S(2)}) %collective-permute-start) | collective-permute-done | bytes 1048608 | tf_op jit(solution)/shard_map/while/body/eval_jaxpr/ppermute | solution.py:29
  293.3 24.0 %while.100 = (s32[]{:T(128)}, f32[2048]{0:T(1024)S(1)}, f32[2048]{0:T(1024)S(1)}, f32[2048,128]{1,0:T(8,128)}, pred[]{:T(512)}, /*index=5*/f32[1024,256]{0,1:T(8...) while((s32[]{:T(128)}, f32[2048]{0:T(1024)S(1)}, ...), condition=%wide.region_15.15_spmd, body=%wide.region_12.14_spmd.sunk | while | flops 1893208064 | bytes 35651772 | solution.py:98
  300.5 4.8 %convolution_add_fusion.6 = f32[2048,128]{1,0:T(8,128)} fusion(f32[512,2048]{1,0:T(8,128)} %copy-done, f32[2048]{0:T(1024)S(1)} %max.48, pred[]{:T(512)} %get-tuple-element.1047, f32[2048,128]{1,0:T(8,128)} %get-tuple-element.1035, f32[2048]{0:T(1024)S(1)} %get-tuple-element.1020, bf16[512,128]{1,0:T(8,128)(2,1)S(1)} %copy.255), kind=kOutput, calls=%fused_computation.33.clone.1 | convolution fusion | flops 274202624 | bytes 6438913 | tf_op jit(solution)/shard_map/while/body/eval_jaxpr/while/body/eval_jaxpr/...ij,...je->...ie/dot_general | solution.py:79
  312.5 4.8 %convolution_add_fusion.6 = f32[2048,128]{1,0:T(8,128)} fusion(f32[512,2048]{1,0:T(8,128)} %copy-done, f32[2048]{0:T(1024)S(1)} %max.48, pred[]{:T(512)} %get-tuple-element.1047, f32[2048,128]{1,0:T(8,128)} %get-tuple-element.1035, f32[2048]{0:T(1024)S(1)} %get-tuple-element.1020, bf16[512,128]{1,0:T(8,128)(2,1)S(1)} %copy.255), kind=kOutput, calls=%fused_computation.33.clone.1 | convolution fusion | flops 274202624 | bytes 6438913 | tf_op jit(solution)/shard_map/while/body/eval_jaxpr/while/body/eval_jaxpr/...ij,...je->...ie/dot_general | solution.py:79
  327.6 5.6 %all-to-all-start.3 = ((f32[1024,2,128]{2,1,0:T(2,128)}), f32[1024,2,128]{2,1,0:T(2,128)}, u32[]{:S(2)}, u32[]{:S(2)}) async-start(f32[1024,2,128]{2,1,0:T(2,128)} %copy.176), calls=%async_computation.3 | async-start | bytes 2097152 | tf_op jit(solution)/shard_map/all_to_all | solution.py:204
  337.8 11.0 %all-to-all-done.3 = f32[1024,2,128]{2,1,0:T(2,128)} async-done(((f32[1024,2,128]{2,1,0:T(2,128)}), f32[1024,2,128]{2,1,0:T(2,128)}, u32[]{:S(2)}, u32[]{:S(2)}) %all-to-all-start.3) | async-done | bytes 1048608 | tf_op jit(solution)/shard_map/all_to_all | solution.py:204
  353.0 51.2 %while.95 = (s32[]{:T(128)}, f32[4,512,128]{1,2,0:T(8,128)S(1)}, f32[4,512]{1,0:T(4,128)S(1)}, f32[4,512]{1,0:T(4,128)S(1)}, f32[4,512,128]{2,1,0:T(8,128)S(1)},...) while((s32[]{:T(128)}, f32[4,512,128]{1,2,0:T(8,128)S(1)}, ...), condition=%wide.region_6.7_spmd, body=%wide.region_3.6_spmd.sunk | while | flops 875302912 | bytes 15991019 | solution.py:157
  (314 shorter events, 169.4 us)
Async XLA Ops:
  6.5 47.1 %copy-start.9 = (bf16[128,4,128]{2,1,0:T(4,128)(2,1)S(1)}, bf16[128,4,128]{2,1,0:T(4,128)(2,1)}, u32[]{:S(2)}) copy-start(bf16[128,4,128]{2,1,0:T(4,128)(2,1)} %param.18) | copy-start | bytes 393220
  6.5 48.6 %copy-start.14 = (bf16[128,16,128]{2,1,0:T(8,128)(2,1)S(1)}, bf16[128,16,128]{2,1,0:T(8,128)(2,1)}, u32[]{:S(2)}) copy-start(bf16[128,16,128]{2,1,0:T(8,128)(2,1)} %param.15) | copy-start | bytes 1572868
  6.5 48.8 %copy-start.16 = (bf16[128,4,128]{2,1,0:T(4,128)(2,1)S(1)}, bf16[128,4,128]{2,1,0:T(4,128)(2,1)}, u32[]{:S(2)}) copy-start(bf16[128,4,128]{2,1,0:T(4,128)(2,1)} %param.17) | copy-start | bytes 393220
  6.5 98.0 %all-gather.4.cloned.1.call-start = ((), (), s32[]{:S(2)}) async-start(), calls=%async_computation.5 | async-start | bytes 2359296 | tf_op jit(solution)/shard_map/all_gather | solution.py:138
  53.6 6.8 %copy-start.7 = (f32[4,128,256]{2,1,0:T(8,128)}, f32[4,128,256]{2,1,0:T(8,128)S(1)}, u32[]{:S(2)}) copy-start(f32[4,128,256]{2,1,0:T(8,128)S(1)} %fusion.49) | copy-start | bytes 1572868
  55.3 52.4 %copy-start.5 = (bf16[128,16,128]{2,0,1:T(8,128)(2,1)}, bf16[128,16,128]{2,0,1:T(8,128)(2,1)S(1)}, u32[]{:S(2)}) copy-start(bf16[128,16,128]{2,0,1:T(8,128)(2,1)S(1)} %copy.148) | copy-start | bytes 1572868
  55.5 49.1 %copy-start.10 = (bf16[128,4,128]{0,2,1:T(8,128)(2,1)}, bf16[128,4,128]{0,2,1:T(8,128)(2,1)S(1)}, u32[]{:S(2)}) copy-start(bf16[128,4,128]{0,2,1:T(8,128)(2,1)S(1)} %copy.204) | copy-start | bytes 393220
  57.0 78.9 %copy-start.13 = (f32[4,128,128]{1,2,0:T(8,128)}, f32[4,128,128]{1,2,0:T(8,128)S(1)}, u32[]{:S(2)}) copy-start(f32[4,128,128]{1,2,0:T(8,128)S(1)} %convolution_subtract_fusion.2) | copy-start | bytes 786436
  60.4 57.2 %copy-start.4 = (f32[4,4,128,128]{3,2,1,0:T(8,128)}, f32[4,4,128,128]{3,2,1,0:T(8,128)S(1)}, u32[]{:S(2)}) copy-start(f32[4,4,128,128]{3,2,1,0:T(8,128)S(1)} %convolution_subtract_fusion.1) | copy-start | bytes 3145732
  119.6 29.2 %all-to-all-start.1 = ((f32[128,8,2,128]{3,0,2,1:T(8,128)}), f32[128,8,2,128]{3,0,2,1:T(8,128)S(1)}, u32[]{:S(2)}, u32[]{:S(2)}) async-start(f32[128,8,2,128]{3,0,2,1:T(8,128)} %bitcast.46), calls=%async_computation.1 | async-start | bytes 2097152 | tf_op jit(solution)/shard_map/all_to_all | solution.py:179
  135.8 20.3 %copy-start.12 = (f32[4,128,128]{2,1,0:T(8,128)S(1)}, f32[4,128,128]{2,1,0:T(8,128)}, u32[]{:S(2)}) copy-start(f32[4,128,128]{2,1,0:T(8,128)} %convolution_subtract_fusion.3) | copy-start | bytes 786436
  149.9 43.8 %all-to-all-start = ((f32[128,8,256]{0,2,1:T(8,128)}), f32[128,8,256]{0,2,1:T(8,128)S(1)}, u32[]{:S(2)}, u32[]{:S(2)}) async-start(f32[128,8,256]{0,2,1:T(8,128)} %bitcast.228), calls=%async_computation | async-start | bytes 2097152 | tf_op jit(solution)/shard_map/all_to_all | solution.py:180
  154.2 198.8 %all-gather.6.cloned.1.call-start = ((), (), s32[]{:S(2)}) async-start(), calls=%async_computation.6 | async-start | bytes 4718592 | tf_op jit(solution)/shard_map/all_gather | solution.py:137
  195.5 16.1 %collective-permute-start = (f32[1024,256]{0,1:T(8,128)S(1)}, f32[1024,256]{0,1:T(8,128)S(1)}, u32[]{:S(2)}, u32[]{:S(2)}) collective-permute-start(f32[1024,256]{0,1:T(8,128)S(1)} %get-tuple-element.1099), channel_id=1, source_target_pairs={{0,8},{8,16},{16,24},{1,9},{9,17},{17,25},{2,10},{10,18},{18,26},{... | collective-permute-start | bytes 3145736 | tf_op jit(solution)/shard_map/while/body/eval_jaxpr/ppermute | solution.py:29
  236.4 16.1 %collective-permute-start = (f32[1024,256]{0,1:T(8,128)S(1)}, f32[1024,256]{0,1:T(8,128)S(1)}, u32[]{:S(2)}, u32[]{:S(2)}) collective-permute-start(f32[1024,256]{0,1:T(8,128)S(1)} %get-tuple-element.1099), channel_id=1, source_target_pairs={{0,8},{8,16},{16,24},{1,9},{9,17},{17,25},{2,10},{10,18},{18,26},{... | collective-permute-start | bytes 3145736 | tf_op jit(solution)/shard_map/while/body/eval_jaxpr/ppermute | solution.py:29
  277.2 16.1 %collective-permute-start = (f32[1024,256]{0,1:T(8,128)S(1)}, f32[1024,256]{0,1:T(8,128)S(1)}, u32[]{:S(2)}, u32[]{:S(2)}) collective-permute-start(f32[1024,256]{0,1:T(8,128)S(1)} %get-tuple-element.1099), channel_id=1, source_target_pairs={{0,8},{8,16},{16,24},{1,9},{9,17},{17,25},{2,10},{10,18},{18,26},{... | collective-permute-start | bytes 3145736 | tf_op jit(solution)/shard_map/while/body/eval_jaxpr/ppermute | solution.py:29
  318.0 15.4 %copy-start.3 = (f32[4,4,128,128]{2,3,1,0:T(8,128)S(1)}, f32[4,4,128,128]{2,3,1,0:T(8,128)}, u32[]{:S(2)}) copy-start(f32[4,4,128,128]{2,3,1,0:T(8,128)} %copy-done.2) | copy-start | bytes 3145732
  318.0 15.4 %copy-start.8 = (f32[4,128,256]{2,1,0:T(8,128)S(1)}, f32[4,128,256]{2,1,0:T(8,128)}, u32[]{:S(2)}) copy-start(f32[4,128,256]{2,1,0:T(8,128)} %copy-done.7) | copy-start | bytes 1572868
  318.7 9.0 %all-to-all-start.2 = ((f32[8,128,2]{1,2,0:T(2,128)}), f32[8,128,2]{1,2,0:T(2,128)S(1)}, u32[]{:S(2)}, u32[]{:S(2)}) async-start(f32[8,128,2]{1,2,0:T(2,128)} %bitcast.53), calls=%async_computation.2 | async-start | bytes 16384 | tf_op jit(solution)/shard_map/all_to_all | solution.py:205
  322.5 12.7 %copy-start.6 = (bf16[128,16,128]{2,0,1:T(8,128)(2,1)S(1)}, bf16[128,16,128]{2,0,1:T(8,128)(2,1)}, u32[]{:S(2)}) copy-start(bf16[128,16,128]{2,0,1:T(8,128)(2,1)} %copy-done.5) | copy-start | bytes 1572868
  322.5 12.7 %copy-start.15 = (bf16[128,4,128]{2,1,0:T(4,128)(2,1)S(1)}, bf16[128,4,128]{2,1,0:T(4,128)(2,1)}, u32[]{:S(2)}) copy-start(bf16[128,4,128]{2,1,0:T(4,128)(2,1)} %param.16) | copy-start | bytes 393220
  327.6 21.2 %all-to-all-start.3 = ((f32[1024,2,128]{2,1,0:T(2,128)}), f32[1024,2,128]{2,1,0:T(2,128)}, u32[]{:S(2)}, u32[]{:S(2)}) async-start(f32[1024,2,128]{2,1,0:T(2,128)} %copy.176), calls=%async_computation.3 | async-start | bytes 2097152 | tf_op jit(solution)/shard_map/all_to_all | solution.py:204
  333.2 3.6 copy-start.11
  348.8 56.9 %all-to-all-start.4 = ((f32[8,128,2]{1,2,0:T(2,128)}), f32[8,128,2]{1,2,0:T(2,128)S(1)}, u32[]{:S(2)}, u32[]{:S(2)}) async-start(f32[8,128,2]{1,2,0:T(2,128)} %bitcast.65), calls=%async_computation.4 | async-start | bytes 16384 | tf_op jit(solution)/shard_map/all_to_all | solution.py:206
  (14 other events, 18.7 us)
Sparse Core Ops, SparseCore 0:
  55.2 49.3 all-gather.3
  157.0 84.8 all-gather.5
where the time goes:
time: 417 us; the launch traced here: 415 us
  waiting for transfers between devices  147 us (35%)
  matrix products  115 us (28%)
  other arithmetic  54.8 us (13%)
  local copies, waits for them, and re-layouts  53.7 us (13%)
  starting transfers between devices  28.6 us (7%)
  between operations  13.9 us (3%)
    all_gather x1, waiting for transfers between devices, body(): lax.all_gather(block_map, 'key', axis=0, tiled=True)  44.1 us
    ppermute x3, waiting for transfers between devices, shifted(): lax.ppermute(value, axis, [(source, source + steps) for source in range(f...  42.5 us
    another operation x3, other arithmetic, block_terms(): lax.linalg.triangular_solve(system, right, left_side=True, lower=True, un...  39.4 us
    all_to_all x1, waiting for transfers between devices, body(): lax.all_to_all(key_slots, 'key', split_axis=1, concat_axis=0, tiled=True)  36.5 us
    dot_general x14, matrix products, attend(): jnp.einsum('...ij,...je->...ie', rounded, values, preferred_element_type=...  34.2 us
    dot_general x6, matrix products, one_block(): jnp.einsum('ie,je->ij', queries_flat, piece[:, :width], precision=highest)  22.7 us
    while x86, local copies, waits for them, and re-layouts  21.6 us
    dot_general x7, matrix products, replay_step(): moving = jnp.einsum('hie,hef->hif', moving, source_map, precision=highest)  14.3 us
  transfers between devices with their start and end apart: 10, of which 8 were waited for; matrix products, arithmetic and copies ran while one was open for 33% of the time, Pallas kernels for 0%

commit v1 on v0

v1 whole, which is shorter than its diff:
```python
import functools

import jax
import jax.numpy as jnp
from jax import lax
from jax.experimental import pallas as pl
from jax.experimental.pallas import tpu as pltpu
from jax.sharding import PartitionSpec as P

F32 = jnp.float32
BF16 = jnp.bfloat16
VMEM_LIMIT = 60 * 1024 * 1024
LOW = -1e30


def halves(x):
    h = x.astype(BF16)
    return h, (x - h.astype(F32)).astype(BF16)


def left_cat(x):
    h, l = halves(x)
    return jnp.concatenate([h, l, h], axis=1)


def right_rows(x):
    h, l = halves(x)
    return jnp.concatenate([h, h, l], axis=0)


def right_cols(x):
    h, l = halves(x)
    return jnp.concatenate([h, h, l], axis=1)


def mm(a, b):
    return lax.dot_general(a, b, (((1,), (0,)), ((), ())), preferred_element_type=F32)


def mm_t(a, b):
    return lax.dot_general(a, b, (((1,), (1,)), ((), ())), preferred_element_type=F32)


def dot_nn(a, b):
    return mm(left_cat(a), right_rows(b))


def dot_nt(a, b):
    return mm_t(left_cat(a), right_cols(b))


def call(kernel, out_shape, args, scratch=(), scalars=None, flops=0, nbytes=0, exps=0):
    vm = pl.BlockSpec(memory_space=pltpu.VMEM)
    sm = pl.BlockSpec(memory_space=pltpu.SMEM)
    specs = [vm] * len(args)
    if scalars is not None:
        specs = [sm] + specs
        args = [scalars] + list(args)
    outs = jax.tree.map(lambda _: vm, out_shape)
    return pl.pallas_call(
        kernel,
        out_shape=out_shape,
        in_specs=specs,
        out_specs=outs,
        scratch_shapes=list(scratch),
        compiler_params=pltpu.CompilerParams(vmem_limit_bytes=VMEM_LIMIT),
        cost_estimate=pl.CostEstimate(flops=flops, bytes_accessed=nbytes, transcendentals=exps),
    )(*args)


def block_kernel(heads, length, width, scal, *refs):
    packs = refs[:heads]
    kt_ref, v_ref, m_ref, wk_ref, yz_ref = refs[heads:]
    place = scal[0]
    rows = lax.broadcasted_iota(jnp.int32, (length, length), 0)
    cols = lax.broadcasted_iota(jnp.int32, (length, length), 1)
    eye = (rows == cols).astype(F32)
    eye_w = (
        lax.broadcasted_iota(jnp.int32, (width, width), 0)
        == lax.broadcasted_iota(jnp.int32, (width, width), 1)
    ).astype(F32)
    strict = rows > cols
    units, keys, betas, lows, xs = [], [], [], [], []
    for d in range(heads):
        k = packs[d][0:length]
        w = packs[d][2 * length : 3 * length]
        b_row = packs[d][3 * length : 3 * length + 1]
        beta = 2.0 / (1.0 + jnp.exp(-b_row))
        beta = jnp.transpose(jnp.broadcast_to(beta, (length, length)))
        unit = w / jnp.sqrt(jnp.sum(w * w, -1, keepdims=True) + 1e-06)
        gram = dot_nt(unit, unit)
        low = jnp.where(strict, beta * gram, 0.0)
        units.append(unit)
        keys.append(k)
        betas.append(beta)
        lows.append(low)
        level = (rows // 2 == cols // 2) & (rows % 2 == 1) & (cols % 2 == 0)
        xs.append(eye - jnp.where(level, low, 0.0))
    size = 2
    while size < length:
        level = (
            (rows // (2 * size) == cols // (2 * size))
            & ((rows // size) % 2 == 1)
            & ((cols // size) % 2 == 0)
        )
        part = [dot_nn(jnp.where(level, lows[d], 0.0), xs[d]) for d in range(heads)]
        part = [dot_nn(xs[d], part[d]) for d in range(heads)]
        xs = [xs[d] - part[d] for d in range(heads)]
        size *= 2
    for d in range(heads):
        slot = lax.rem(place - d + heads, heads)
        unit, k, beta = units[d], keys[d], betas[d]
        kb = k.astype(BF16)
        uh, ul = halves(unit)
        cross = mm_t(jnp.concatenate([uh, ul], axis=1), jnp.concatenate([kb, kb], axis=1))
        cross = jnp.where(strict, cross, 0.0)
        yz = dot_nn(xs[d], jnp.concatenate([beta[:, :width] * unit, beta * cross], axis=1))
        y, z = yz[:, :width], yz[:, width:]
        m_ref[slot] = eye_w - dot_nn(jnp.transpose(unit), y)
        kt_ref[slot] = k - dot_nn(jnp.transpose(z), unit)
        v_ref[slot] = packs[d][length : 2 * length]
        wk_ref[slot] = jnp.concatenate(
            [
                jnp.concatenate([uh, ul], axis=1),
                jnp.concatenate([kb, jnp.zeros_like(kb)], axis=1),
            ],
            axis=0,
        )
        yz_ref[slot] = right_rows(yz)


def section_kernel(heads, ring, width, scal, *refs):
    kts, vs, ms = refs[:ring], refs[ring : 2 * ring], refs[2 * ring : 3 * ring]
    kcat_ref, mcat_ref, vb_ref, kend_ref, vsec_ref, s_ref = refs[3 * ring : 3 * ring + 6]
    kt_s, m_s = refs[3 * ring + 6 :]
    low = scal[1]
    for r in range(ring):
        lane = lax.rem(low - r + ring, ring)
        for t in range(heads):
            b = t * ring + lane
            kt_s[b] = kts[r][t]
            vb_ref[b] = vs[r][t].astype(BF16)
            vsec_ref[b] = vs[r][t]
            kcat_ref[b] = right_cols(kts[r][t])
            mcat_ref[b] = right_rows(ms[r][t])
    eye = (
        lax.broadcasted_iota(jnp.int32, (width, width), 0)
        == lax.broadcasted_iota(jnp.int32, (width, width), 1)
    ).astype(F32)

    last = heads * ring - 1
    m_s[last] = eye

    def step(i, c):
        b = last - i
        m_s[b - 1] = mm(left_cat(m_s[b]), mcat_ref[b])
        return c

    lax.fori_loop(0, last, step, 0)
    s_ref[...] = mm(left_cat(m_s[0]), mcat_ref[0])

    def turn(b, c):
        kend_ref[b] = dot_nt(kt_s[b], m_s[b])
        return c

    lax.fori_loop(0, heads * ring, turn, 0)


def near_kernel(heads, ring, length, width, scal, *refs):
    qs = refs[:heads]
    wk_ref, yz_ref, kcat_ref, mcat_ref, vb_ref = refs[heads : heads + 5]
    qcat_ref, ml_ref, acc_ref = refs[heads + 5 : heads + 8]
    q_s, m_s, l_s = refs[heads + 8 :]
    place, low = scal[0], scal[1]
    rows = qs[0].shape[0]
    scale = width ** (-0.5)
    for d in range(heads):
        q_s[lax.rem(place - d + heads, heads)] = qs[d][...]
    token = lax.rem(lax.broadcasted_iota(jnp.int32, (rows, length), 0), length)
    causal = token >= lax.broadcasted_iota(jnp.int32, (rows, length), 1)

    def own(t, b):
        qf = q_s[t]
        q = qf.astype(BF16)
        both = mm_t(jnp.concatenate([q, q], axis=1), wk_ref[t])
        qw = jnp.where(causal, both[:, :length], 0.0)
        u = mm(left_cat(qw), yz_ref[t])
        q_s[t] = (qf - u[:, :width]) * scale
        s = jnp.where(causal, (both[:, length:] - u[:, width:]) * scale, LOW)
        top = jnp.max(s, -1, keepdims=True)
        p = jnp.where(causal, jnp.exp(s - top), 0.0)
        m_s[t] = top
        l_s[t] = jnp.sum(p, -1, keepdims=True)
        acc_ref[t] = mm(p.astype(BF16), vb_ref[b])

    def earlier(t, b):
        qc = left_cat(q_s[t])
        s = mm_t(qc, kcat_ref[b])
        old = m_s[t]
        top = jnp.maximum(old, jnp.max(s, -1, keepdims=True))
        p = jnp.exp(s - top)
        f = jnp.exp(old - top)
        m_s[t] = top
        l_s[t] = l_s[t] * f + jnp.sum(p, -1, keepdims=True)
        acc_ref[t] = acc_ref[t] * f + mm(p.astype(BF16), vb_ref[b])
        q_s[t] = mm(qc, mcat_ref[b])

    def step(i, carry):
        b = heads * ring - 1 - i
        t_b = b // ring
        lane = b - t_b * ring
        first = jnp.where(low > lane, t_b, t_b + 1)

        def body(t, c):
            earlier(t, b)
            return c

        lax.fori_loop(first, heads, body, 0)

        @pl.when(lane == low)
        def _():
            own(t_b, b)

        return carry

    lax.fori_loop(0, heads * ring, step, 0)

    def finish(t, c):
        qcat_ref[t] = left_cat(q_s[t])
        lane_id = lax.broadcasted_iota(jnp.int32, (rows, 128), 1)
        ml_ref[t] = jnp.where(lane_id < 64, m_s[t], l_s[t])
        return c

    lax.fori_loop(0, heads, finish, 0)


def move_kernel(k_ref, s_ref, out_ref):
    cat = right_cols(s_ref[...])

    def step(b, c):
        out_ref[b] = mm_t(left_cat(k_ref[b]), cat)
        return c

    lax.fori_loop(0, k_ref.shape[0], step, 0)


def far_kernel(step, last, tile, scal, q_ref, ml_ref, acc_ref, k_ref, v_ref, *refs):
    if last:
        out_ref, kc, vc = refs
    else:
        ml_out, acc_out, kc, vc = refs
    blocks, length, width = k_ref.shape
    rows = q_ref.shape[1]
    live = scal[2] >= step

    @pl.when(live)
    def _():
        def prep(b, c):
            at = pl.ds(pl.multiple_of(b * length, length), length)
            kc[at] = right_cols(k_ref[b])
            vc[at] = v_ref[b].astype(BF16)
            return c

        lax.fori_loop(0, blocks, prep, 0)

    per = rows // tile

    def body(i, c):
        t = i // per
        at = pl.ds(pl.multiple_of((i - t * per) * tile, tile), tile)
        ml = ml_ref[t, at]
        old, tot = ml[:, 0:1], ml[:, 64:65]
        acc = acc_ref[t, at]

        def store(m, l, a):
            if last:
                out_ref[t, at] = a / l
            else:
                lane_id = lax.broadcasted_iota(jnp.int32, (tile, 128), 1)
                ml_out[t, at] = jnp.where(lane_id < 64, m, l)
                acc_out[t, at] = a

        @pl.when(live)
        def _():
            s = mm_t(q_ref[t, at], kc[...])
            top = jnp.maximum(old, jnp.max(s, -1, keepdims=True))
            p = jnp.exp(s - top)
            f = jnp.exp(old - top)
            store(
                top,
                tot * f + jnp.sum(p, -1, keepdims=True),
                acc * f + mm(p.astype(BF16), vc[...]),
            )

        @pl.when(jnp.logical_not(live))
        def _():
            store(old, tot, acc)

        return c

    lax.fori_loop(0, q_ref.shape[0] * per, body, 0)


def join_kernel(heads, scal, *refs):
    out_ref = refs[heads]
    for d in range(heads):
        out_ref[lax.rem(scal[0] - d + heads, heads)] = refs[d][...].astype(BF16)


def body(query, key, value, raw_directions, beta_raw_logits):
    length, q_count, width = query.shape
    heads = key.shape[1]
    group = q_count // heads
    key_count, sec_count = lax.axis_size("key"), lax.axis_size("sec")
    ring = key_count // heads
    key_index, sec_index = lax.axis_index("key"), lax.axis_index("sec")
    place, low = key_index // ring, key_index % ring
    scal = jnp.stack([place, low, sec_index]).astype(jnp.int32)
    blocks = heads * ring
    rows = group * length

    def around(d):
        return [(k, ((k // ring + d) % heads) * ring + k % ring) for k in range(key_count)]

    def across(d):
        return [(k, (k // ring) * ring + (k % ring + d) % ring) for k in range(key_count)]

    def spread(x):
        own = [
            lax.dynamic_index_in_dim(x, lax.rem(place + d, heads), 0, keepdims=False)
            for d in range(heads)
        ]
        return [own[0]] + [lax.ppermute(own[d], "key", around(d)) for d in range(1, heads)]

    def by_head(x):
        return jnp.transpose(x.astype(F32), (1, 0, 2))

    sds = jax.ShapeDtypeStruct
    lines = jnp.transpose(beta_raw_logits, (1, 0))[:, None, :]
    lines = jnp.pad(lines, ((0, 0), (0, 7), (0, 0)))
    pack = jnp.concatenate([by_head(key), by_head(value), by_head(raw_directions), lines], axis=1)
    packs = spread(pack)
    q_heads = by_head(query).reshape(heads, rows, width)
    qs = spread(q_heads)

    cube = sds((heads, length, width), F32)
    kt, v, m, wk, yz = call(
        functools.partial(block_kernel, heads, length, width),
        (
            cube,
            cube,
            sds((heads, width, width), F32),
            sds((heads, 2 * length, 2 * width), BF16),
            sds((heads, 3 * length, width + length), BF16),
        ),
        packs,
        scalars=scal,
        flops=heads * 20 * 6 * length**3,
        nbytes=heads * 10 * length * width * 4,
    )

    def gather(x):
        return [x] + [lax.ppermute(x, "key", across(d)) for d in range(1, ring)]

    kts, vs, ms = gather(kt), gather(v), gather(m)
    full = sds((blocks, length, width), F32)
    kcat, mcat, vb, kend, vsec, smap = call(
        functools.partial(section_kernel, heads, ring, width),
        (
            sds((blocks, length, 3 * width), BF16),
            sds((blocks, 3 * width, width), BF16),
            sds((blocks, length, width), BF16),
            full,
            full,
            sds((width, width), F32),
        ),
        kts + vs + ms,
        scratch=[pltpu.VMEM((blocks, length, width), F32)] * 2,
        scalars=scal,
        flops=blocks * 12 * length**3,
        nbytes=blocks * 8 * length * width * 4,
    )
    qcat, ml, acc = call(
        functools.partial(near_kernel, heads, ring, length, width),
        (
            sds((heads, rows, 3 * width), BF16),
            sds((heads, rows, 128), F32),
            sds((heads, rows, width), F32),
        ),
        qs + [wk, yz, kcat, mcat, vb],
        scratch=[
            pltpu.VMEM((heads, rows, width), F32),
            pltpu.VMEM((heads, rows, 1), F32),
            pltpu.VMEM((heads, rows, 1), F32),
        ],
        scalars=scal,
        flops=heads * blocks // 2 * rows * width * length * 14,
        nbytes=heads * rows * width * 16,
        exps=heads * blocks // 2 * rows * length,
    )
    walk = [(s, s + 1) for s in range(sec_count - 1)]
    k_far, v_far = kend, vsec
    for step in range(1, sec_count):
        k_far = lax.ppermute(k_far, "sec", walk)
        v_far = lax.ppermute(v_far, "sec", walk)
        last = step == sec_count - 1
        outs = (sds((heads, rows, 128), F32), sds((heads, rows, width), F32))
        got = call(
            functools.partial(far_kernel, step, last, 256),
            outs[1] if last else outs,
            [qcat, ml, acc, k_far, v_far],
            scratch=[
                pltpu.VMEM((blocks * length, 3 * width), BF16),
                pltpu.VMEM((blocks * length, width), BF16),
            ],
            scalars=scal,
            flops=heads * rows * blocks * length * width * 8,
            nbytes=heads * rows * width * 16,
            exps=heads * rows * blocks * length,
        )
        if last:
            out = got
        else:
            ml, acc = got
            k_far = call(
                move_kernel,
                full,
                [k_far, smap],
                flops=blocks * 6 * length**3,
                nbytes=blocks * length * width * 8,
            )
    back = spread(out)
    joined = call(
        functools.partial(join_kernel, heads),
        sds((heads, rows, width), BF16),
        back,
        scalars=scal,
        nbytes=heads * rows * width * 6,
    )
    return jnp.transpose(joined.reshape(q_count, length, width), (1, 0, 2))


def solution(mesh):
    rows = P(("sec", "key"), None, None)
    return jax.shard_map(
        body,
        mesh=mesh,
        in_specs=(rows, rows, rows, rows, P(("sec", "key"), None)),
        out_specs=rows,
        check_vma=False,
    )
```

time: 417 us -> 175 us (0.42)
  matrix products: 115 us -> 0 us
  waiting for transfers between devices: 147 us -> 59.8 us
  Pallas kernels: 0 us -> 67.5 us
  other arithmetic: 54.8 us -> 3.49 us
  local copies, waits for them, and re-layouts: 53.7 us -> 12 us
  between operations: 13.9 us -> 0.2 us
    dot_general x63 -> x0, matrix products: 114 us -> none  [the longest x14 34.2 us: attend(): jnp.einsum('...ij,...je->...ie', rounded, values, preferred_element_type=...]
    pallas_call x0 -> x9, Pallas kernels: none -> 67.5 us  [call(): pl.pallas_call(kernel, out_shape=out_shape, in_specs=specs, out_specs=out...]
    all_to_all x5 -> x0, waiting for transfers between devices: 60.3 us -> none  [the longest x1 36.5 us: body(): lax.all_to_all(key_slots, 'key', split_axis=1, concat_axis=0, tiled=True)]
    all_gather x2 -> x0, waiting for transfers between devices: 44.1 us -> none  [the longest x1 44.1 us: body(): lax.all_gather(block_map, 'key', axis=0, tiled=True)]
    another operation x5 -> x1, other arithmetic: 39.4 us -> 0.58 us  [body(): scal = jnp.stack([place, low, sec_index]).astype(jnp.int32)]
    ppermute x3 -> x18, starting transfers between devices: 5.75 us -> 29.5 us  [the longest x9 15.5 us: spread(): lax.ppermute(own[d], 'key', around(d))]
    while x88 -> x0, local copies, waits for them, and re-layouts: 23.5 us -> none
    all_to_all x5 -> x0, starting transfers between devices: 22.9 us -> none  [the longest x1 5.6 us: body(): lax.all_to_all(far_sums, 'key', split_axis=0, concat_axis=1, tiled=True)]
  transfers between devices with their start and end apart: 10 -> 18, of which waited for: 8 -> 9; matrix products, arithmetic and copies ran while one was open for 33% -> 1% of each run, Pallas kernels for 0% -> 28%
where the time goes in v1:
time: 175 us; the launch traced here: 172 us
  Pallas kernels  67.5 us (39%)
  waiting for transfers between devices  59.8 us (34%)
  starting transfers between devices  29.5 us (17%)
  local copies, waits for them, and re-layouts  12 us (7%)
  other arithmetic  3.49 us (2%)
    pallas_call x9, Pallas kernels, call(): pl.pallas_call(kernel, out_shape=out_shape, in_specs=specs, out_specs=out...  67.5 us
    ppermute x9, waiting for transfers between devices, spread(): lax.ppermute(own[d], 'key', around(d))  36.8 us
    ppermute x3, waiting for transfers between devices, gather(): return [x] + [lax.ppermute(x, 'key', across(d)) for d in range(1, ring)]  16.1 us
    ppermute x9, starting transfers between devices, spread(): lax.ppermute(own[d], 'key', around(d))  15.5 us
    ppermute x3, waiting for transfers between devices, body(): k_far = lax.ppermute(k_far, 'sec', walk)  6.86 us
    ppermute x3, starting transfers between devices, body(): v_far = lax.ppermute(v_far, 'sec', walk)  5.76 us
    ppermute x3, starting transfers between devices, body(): k_far = lax.ppermute(k_far, 'sec', walk)  5.72 us
    unnamed x38, local copies, waits for them, and re-layouts  5.65 us
  transfers between devices with their start and end apart: 18, of which 9 were waited for; matrix products, arithmetic and copies ran while one was open for 1% of the time, Pallas kernels for 28%

profile of v1, /device:TPU:6, one launch (start us, length us, event | category | flops | bytes accessed | tf_op | source)
XLA Modules:
  0.0 172.4 jit_solution(10765615087995238683)
XLA Ops:
  4.2 2.6 %collective-permute-start.4 = (f32[392,128]{1,0:T(8,128)S(1)}, f32[392,128]{1,0:T(8,128)S(1)}, u32[]{:S(2)}, u32[]{:S(2)}) collective-permute-start(f32[392,128]{1,0:T(8,128)S(1)} %bitcast.44), channel_id=1, source_target_pairs={{0,4},{1,5},{2,6},{3,7},{4,0},{5,1},{6,2},{7,3},{8,12},{9,13},{10,... | collective-permute-start | bytes 602120 | tf_op jit(solution)/shard_map/ppermute | solution.py:333
  9.4 9.0 %collective-permute-done.4.refs_2_ = f32[392,128]{1,0:T(8,128)S(1)} collective-permute-done((f32[392,128]{1,0:T(8,128)S(1)}, f32[392,128]{1,0:T(8,128)S(1)}, u32[]{:S(2)}, u32[]{:S(2)}) %collective-permute-start.4) | collective-permute-done | bytes 200736 | tf_op jit(solution)/shard_map/ppermute | solution.py:333
  18.4 3.2 %collective-permute-done.3.refs_1_ = f32[392,128]{1,0:T(8,128)S(1)} collective-permute-done((f32[392,128]{1,0:T(8,128)S(1)}, f32[392,128]{1,0:T(8,128)S(1)}, u32[]{:S(2)}, u32[]{:S(2)}) %collective-permute-start.3) | collective-permute-done | bytes 200736 | tf_op jit(solution)/shard_map/ppermute | solution.py:333
  22.3 6.5 %shard_map.55 = (f32[4,128,128]{2,1,0:T(8,128)}, f32[4,128,128]{2,1,0:T(8,128)}, f32[4,128,128]{2,1,0:T(8,128)}, bf16[4,256,256]{2,1,0:T(8,128)(2,1)}, bf16[4,384,256]{2,1,0:T(8,128)(2,1)}) custom-call(s32[3]{0:T(128)} %pad_add_fusion.scal, f32[392,128]{1,0:T(8,128)} %bitcast.41, f32[392,128]{1,0:T(8,128)} %copy-done.18, f32[392,128]{1,0:T(8,128)} %copy-done.16, ...), custom_call_target="tpu_custom_call" | custom-call | flops 1006632960 | bytes 2621440 | tf_op jit(solution)/shard_map/pallas_call | solution.py:60
  31.3 6.9 %collective-permute-done.6.refs_1_ = f32[4,128,128]{2,1,0:T(8,128)S(1)} collective-permute-done((f32[4,128,128]{2,1,0:T(8,128)}, f32[4,128,128]{2,1,0:T(8,128)S(1)}, u32[]{:S(2)}, u32[]{:S(2)}) %collective-permute-start.6) | collective-permute-done | bytes 262176 | tf_op jit(solution)/shard_map/ppermute | solution.py:363
  38.2 5.6 %collective-permute-done.7.refs_3_ = f32[4,128,128]{2,1,0:T(8,128)S(1)} collective-permute-done((f32[4,128,128]{2,1,0:T(8,128)}, f32[4,128,128]{2,1,0:T(8,128)S(1)}, u32[]{:S(2)}, u32[]{:S(2)}) %collective-permute-start.7) | collective-permute-done | bytes 262176 | tf_op jit(solution)/shard_map/ppermute | solution.py:363
  43.8 3.6 %collective-permute-done.8.refs_5_ = f32[4,128,128]{2,1,0:T(8,128)S(1)} collective-permute-done((f32[4,128,128]{2,1,0:T(8,128)}, f32[4,128,128]{2,1,0:T(8,128)S(1)}, u32[]{:S(2)}, u32[]{:S(2)}) %collective-permute-start.8) | collective-permute-done | bytes 262176 | tf_op jit(solution)/shard_map/ppermute | solution.py:363
  48.1 5.9 %shard_map.56 = (bf16[8,128,384]{2,1,0:T(8,128)(2,1)}, bf16[8,384,128]{2,1,0:T(8,128)(2,1)}, bf16[8,128,128]{2,1,0:T(8,128)(2,1)}, f32[8,128,128]{2,1,0:T(8,128)...) custom-call(s32[3]{0:T(128)} %pad_add_fusion.scal, f32[4,128,128]{2,1,0:T(8,128)} %get-tuple-element.25.refs_0_, ...), custom_call_target="tpu_custom_call" | custom-call | flops 201326592 | bytes 4194304 | tf_op jit(solution)/shard_map/pallas_call | solution.py:60
  57.9 6.9 %collective-permute-done.9.k_ref = f32[8,128,128]{2,1,0:T(8,128)S(1)} collective-permute-done((f32[8,128,128]{2,1,0:T(8,128)}, f32[8,128,128]{2,1,0:T(8,128)S(1)}, u32[]{:S(2)}, u32[]{:S(2)}) %collective-permute-start.9) | collective-permute-done | bytes 524320 | tf_op jit(solution)/shard_map/ppermute | solution.py:404
  65.6 3.4 %shard_map.59 = f32[8,128,128]{2,1,0:T(8,128)} custom-call(f32[8,128,128]{2,1,0:T(8,128)} %copy-done.1, f32[128,128]{1,0:T(8,128)} %get-tuple-element.38.s_ref), custom_call_target="tpu_custom_call" | custom-call | flops 100663296 | bytes 1048576 | tf_op jit(solution)/shard_map/pallas_call | solution.py:60
  73.7 3.6 %collective-permute-start.2 = (f32[512,128]{1,0:T(8,128)S(1)}, f32[512,128]{1,0:T(8,128)S(1)}, u32[]{:S(2)}, u32[]{:S(2)}) collective-permute-start(f32[512,128]{1,0:T(8,128)S(1)} %get-tuple-element.45), channel_id=1, source_target_pairs={{0,6},{1,7},{2,0},{3,1},{4,2},{5,3},{6,4},{7,5},{8,14},{9,15},{10,... | collective-permute-start | bytes 786440 | tf_op jit(solution)/shard_map/ppermute | solution.py:333
  77.3 3.2 %collective-permute-start.1 = (f32[512,128]{1,0:T(8,128)S(1)}, f32[512,128]{1,0:T(8,128)S(1)}, u32[]{:S(2)}, u32[]{:S(2)}) collective-permute-start(f32[512,128]{1,0:T(8,128)S(1)} %get-tuple-element.46), channel_id=1, source_target_pairs={{0,4},{1,5},{2,6},{3,7},{4,0},{5,1},{6,2},{7,3},{8,12},{9,13},{10,... | collective-permute-start | bytes 786440 | tf_op jit(solution)/shard_map/ppermute | solution.py:333
  80.6 2.0 %collective-permute-start = (f32[512,128]{1,0:T(8,128)S(1)}, f32[512,128]{1,0:T(8,128)S(1)}, u32[]{:S(2)}, u32[]{:S(2)}) collective-permute-start(f32[512,128]{1,0:T(8,128)S(1)} %get-tuple-element.47), channel_id=1, source_target_pairs={{0,2},{1,3},{2,4},{3,5},{4,6},{5,7},{6,0},{7,1},{8,10},{9,11},{10,... | collective-permute-start | bytes 786440 | tf_op jit(solution)/shard_map/ppermute | solution.py:333
  83.4 3.4 %shard_map.61 = f32[8,128,128]{2,1,0:T(8,128)} custom-call(f32[8,128,128]{2,1,0:T(8,128)} %copy-done.2, f32[128,128]{1,0:T(8,128)} %get-tuple-element.38.s_ref), custom_call_target="tpu_custom_call" | custom-call | flops 100663296 | bytes 1048576 | tf_op jit(solution)/shard_map/pallas_call | solution.py:60
  90.6 5.4 %collective-permute-done.1.refs_2_ = f32[512,128]{1,0:T(8,128)S(1)} collective-permute-done((f32[512,128]{1,0:T(8,128)S(1)}, f32[512,128]{1,0:T(8,128)S(1)}, u32[]{:S(2)}, u32[]{:S(2)}) %collective-permute-start.1) | collective-permute-done | bytes 262176 | tf_op jit(solution)/shard_map/ppermute | solution.py:333
  96.8 18.5 %shard_map.57 = (bf16[4,512,384]{2,1,0:T(8,128)(2,1)}, f32[4,512,128]{2,1,0:T(8,128)}, f32[4,512,128]{2,1,0:T(8,128)}) custom-call(s32[3]{0:T(128)} %pad_add_fusion.scal, f32[512,128]{1,0:T(8,128)} %get-tuple-element.48.refs_0_, f32[512,128]{1,0:T(8,128)} %copy-done.15, f32[512,128]{1,0:T(8,128)} %copy-done.14, f32[512,128]{1,0:T(8,128)} %copy-done.13, ...), custom_call_target="tpu_custom_call" | custom-call | flops 1879048192 | bytes 4194304 | tf_op jit(solution)/shard_map/pallas_call | solution.py:60
  115.3 11.7 %shard_map.58 = (f32[4,512,128]{2,1,0:T(8,128)}, f32[4,512,128]{2,1,0:T(8,128)}) custom-call(s32[3]{0:T(128)} %pad_add_fusion.scal, bf16[4,512,384]{2,1,0:T(8,128)(2,1)} %get-tuple-element.31.q_ref, f32[4,512,128]{2,1,0:T(8,128)} %get-tuple-element.32.ml_ref, f32[4,512,128]{2,1,0:T(8,128)} %get-tuple-element.33.acc_ref, f32[8,128,128]{2,1,0:T(8,128)} %copy-done.1, ...), custom_call_target="tpu_custom_call" | custom-call | flops 2147483648 | bytes 4194304 | tf_op jit(solution)/shard_map/pallas_call | solution.py:60
  127.1 11.7 %shard_map.60 = (f32[4,512,128]{2,1,0:T(8,128)}, f32[4,512,128]{2,1,0:T(8,128)}) custom-call(s32[3]{0:T(128)} %pad_add_fusion.scal, bf16[4,512,384]{2,1,0:T(8,128)(2,1)} %get-tuple-element.31.q_ref, f32[4,512,128]{2,1,0:T(8,128)} %get-tuple-element.36.ml_ref, f32[4,512,128]{2,1,0:T(8,128)} %get-tuple-element.37.acc_ref, f32[8,128,128]{2,1,0:T(8,128)} %copy-done.2, ...), custom_call_target="tpu_custom_call" | custom-call | flops 2147483648 | bytes 4194304 | tf_op jit(solution)/shard_map/pallas_call | solution.py:60
  139.8 4.4 %shard_map.62 = f32[4,512,128]{2,1,0:T(8,128)} custom-call(s32[3]{0:T(128)} %pad_add_fusion.scal, bf16[4,512,384]{2,1,0:T(8,128)(2,1)} %get-tuple-element.31.q_ref, f32[4,512,128]{2,1,0:T(8,128)} %get-tuple-element.39.ml_ref, f32[4,512,128]{2,1,0:T(8,128)} %get-tuple-element.40.acc_ref, f32[8,128,128]{2,1,0:T(8,128)} %copy-done.11, f32[8,128,128]{2,1,0:T(8,128)} %copy-done.12), custom_call_target="tpu_custom_call" | custom-call | flops 2147483648 | bytes 4194304 | tf_op jit(solution)/shard_map/pallas_call | solution.py:60
  146.1 2.0 %collective-permute-start.15 = (f32[512,128]{1,0:T(8,128)S(1)}, f32[512,128]{1,0:T(8,128)S(1)}, u32[]{:S(2)}, u32[]{:S(2)}) collective-permute-start(f32[512,128]{1,0:T(8,128)S(1)} %get-tuple-element.43), channel_id=1, source_target_pairs={{0,2},{1,3},{2,4},{3,5},{4,6},{5,7},{6,0},{7,1},{8,10},{9,11},{10,... | collective-permute-start | bytes 786440 | tf_op jit(solution)/shard_map/ppermute | solution.py:333
  148.1 7.6 %collective-permute-done.17.refs_3_ = f32[512,128]{1,0:T(8,128)S(1)} collective-permute-done((f32[512,128]{1,0:T(8,128)S(1)}, f32[512,128]{1,0:T(8,128)S(1)}, u32[]{:S(2)}, u32[]{:S(2)}) %collective-permute-start.17) | collective-permute-done | bytes 262176 | tf_op jit(solution)/shard_map/ppermute | solution.py:333
  155.7 11.7 %collective-permute-done.16.refs_2_ = f32[512,128]{1,0:T(8,128)S(1)} collective-permute-done((f32[512,128]{1,0:T(8,128)S(1)}, f32[512,128]{1,0:T(8,128)S(1)}, u32[]{:S(2)}, u32[]{:S(2)}) %collective-permute-start.16) | collective-permute-done | bytes 262176 | tf_op jit(solution)/shard_map/ppermute | solution.py:333
  168.2 2.0 %shard_map.63 = bf16[4,512,128]{2,1,0:T(8,128)(2,1)} custom-call(s32[3]{0:T(128)} %pad_add_fusion.scal, f32[512,128]{1,0:T(8,128)} %get-tuple-element.44.refs_0_, f32[512,128]{1,0:T(8,128)} %copy-done.8, f32[512,128]{1,0:T(8,128)} %copy-done.7, f32[512,128]{1,0:T(8,128)} %copy-done.5), custom_call_target="tpu_custom_call" | custom-call | bytes 1572864 | tf_op jit(solution)/shard_map/pallas_call | solution.py:60
  170.3 2.2 %copy.11 = bf16[16,128,128]{2,0,1:T(8,128)(2,1)} copy(bf16[16,128,128]{2,1,0:T(8,128)(2,1)} %bitcast.40) | data formatting | bytes 1048576 | tf_op jit(solution)/shard_map/reshape | solution.py:440
  (68 shorter events, 29.3 us)
Async XLA Ops:
  4.2 14.2 %collective-permute-start.4 = (f32[392,128]{1,0:T(8,128)S(1)}, f32[392,128]{1,0:T(8,128)S(1)}, u32[]{:S(2)}, u32[]{:S(2)}) collective-permute-start(f32[392,128]{1,0:T(8,128)S(1)} %bitcast.44), channel_id=1, source_target_pairs={{0,4},{1,5},{2,6},{3,7},{4,0},{5,1},{6,2},{7,3},{8,12},{9,13},{10,... | collective-permute-start | bytes 602120 | tf_op jit(solution)/shard_map/ppermute | solution.py:333
  6.8 11.6 %collective-permute-start.5 = (f32[392,128]{1,0:T(8,128)S(1)}, f32[392,128]{1,0:T(8,128)S(1)}, u32[]{:S(2)}, u32[]{:S(2)}) collective-permute-start(f32[392,128]{1,0:T(8,128)S(1)} %bitcast.43), channel_id=1, source_target_pairs={{0,6},{1,7},{2,0},{3,1},{4,2},{5,3},{6,4},{7,5},{8,14},{9,15},{10,... | collective-permute-start | bytes 602120 | tf_op jit(solution)/shard_map/ppermute | solution.py:333
  8.2 13.4 %collective-permute-start.3 = (f32[392,128]{1,0:T(8,128)S(1)}, f32[392,128]{1,0:T(8,128)S(1)}, u32[]{:S(2)}, u32[]{:S(2)}) collective-permute-start(f32[392,128]{1,0:T(8,128)S(1)} %bitcast.42), channel_id=1, source_target_pairs={{0,2},{1,3},{2,4},{3,5},{4,6},{5,7},{6,0},{7,1},{8,10},{9,11},{10,... | collective-permute-start | bytes 602120 | tf_op jit(solution)/shard_map/ppermute | solution.py:333
  28.8 44.0 %copy-start = (bf16[128,16,128]{2,1,0:T(8,128)(2,1)S(1)}, bf16[128,16,128]{2,1,0:T(8,128)(2,1)}, u32[]{:S(2)}) copy-start(bf16[128,16,128]{2,1,0:T(8,128)(2,1)} %param.5) | copy-start | bytes 1572868
  28.8 9.4 %collective-permute-start.6 = (f32[4,128,128]{2,1,0:T(8,128)}, f32[4,128,128]{2,1,0:T(8,128)S(1)}, u32[]{:S(2)}, u32[]{:S(2)}) collective-permute-start(f32[4,128,128]{2,1,0:T(8,128)} %get-tuple-element.25.refs_0_), channel_id=1, source_target_pairs={{0,1},{1,0},{2,3},{3,2},{4,5},{5,4},{6,7},{7,6},{8,9},{9,8},{10,11... | collective-permute-start | bytes 786440 | tf_op jit(solution)/shard_map/ppermute | solution.py:363
  29.3 14.5 %collective-permute-start.7 = (f32[4,128,128]{2,1,0:T(8,128)}, f32[4,128,128]{2,1,0:T(8,128)S(1)}, u32[]{:S(2)}, u32[]{:S(2)}) collective-permute-start(f32[4,128,128]{2,1,0:T(8,128)} %get-tuple-element.26.refs_2_), channel_id=1, source_target_pairs={{0,1},{1,0},{2,3},{3,2},{4,5},{5,4},{6,7},{7,6},{8,9},{9,8},{10,11... | collective-permute-start | bytes 786440 | tf_op jit(solution)/shard_map/ppermute | solution.py:363
  30.8 16.6 %collective-permute-start.8 = (f32[4,128,128]{2,1,0:T(8,128)}, f32[4,128,128]{2,1,0:T(8,128)S(1)}, u32[]{:S(2)}, u32[]{:S(2)}) collective-permute-start(f32[4,128,128]{2,1,0:T(8,128)} %get-tuple-element.27.refs_4_), channel_id=1, source_target_pairs={{0,1},{1,0},{2,3},{3,2},{4,5},{5,4},{6,7},{7,6},{8,9},{9,8},{10,11... | collective-permute-start | bytes 786440 | tf_op jit(solution)/shard_map/ppermute | solution.py:363
  38.2 9.2 %copy-start.3 = (f32[4,128,128]{2,1,0:T(8,128)}, f32[4,128,128]{2,1,0:T(8,128)S(1)}, u32[]{:S(2)}) copy-start(f32[4,128,128]{2,1,0:T(8,128)S(1)} %collective-permute-done.6.refs_1_) | copy-start | bytes 786436
  43.8 3.6 %copy-start.4 = (f32[4,128,128]{2,1,0:T(8,128)}, f32[4,128,128]{2,1,0:T(8,128)S(1)}, u32[]{:S(2)}) copy-start(f32[4,128,128]{2,1,0:T(8,128)S(1)} %collective-permute-done.7.refs_3_) | copy-start | bytes 786436
  54.1 10.7 %collective-permute-start.9 = (f32[8,128,128]{2,1,0:T(8,128)}, f32[8,128,128]{2,1,0:T(8,128)S(1)}, u32[]{:S(2)}, u32[]{:S(2)}) collective-permute-start(f32[8,128,128]{2,1,0:T(8,128)} %get-tuple-element.34), channel_id=1, source_target_pairs={{0,8},{8,16},{16,24},{1,9},{9,17},{17,25},{2,10},{10,18},{18,26},{... | collective-permute-start | bytes 1572872 | tf_op jit(solution)/shard_map/ppermute | solution.py:404
  56.0 14.9 %collective-permute-start.10 = (f32[8,128,128]{2,1,0:T(8,128)}, f32[8,128,128]{2,1,0:T(8,128)S(1)}, u32[]{:S(2)}, u32[]{:S(2)}) collective-permute-start(f32[8,128,128]{2,1,0:T(8,128)} %get-tuple-element.35), channel_id=1, source_target_pairs={{0,8},{8,16},{16,24},{1,9},{9,17},{17,25},{2,10},{10,18},{18,26},{... | collective-permute-start | bytes 1572872 | tf_op jit(solution)/shard_map/ppermute | solution.py:405
  68.9 13.6 %collective-permute-start.11 = (f32[8,128,128]{2,1,0:T(8,128)}, f32[8,128,128]{2,1,0:T(8,128)S(1)}, u32[]{:S(2)}, u32[]{:S(2)}) collective-permute-start(f32[8,128,128]{2,1,0:T(8,128)} %shard_map.59), channel_id=1, source_target_pairs={{0,8},{8,16},{16,24},{1,9},{9,17},{17,25},{2,10},{10,18},{18,26},{... | collective-permute-start | bytes 1572872 | tf_op jit(solution)/shard_map/ppermute | solution.py:404
  70.9 17.8 %collective-permute-start.12 = (f32[8,128,128]{2,1,0:T(8,128)S(1)}, f32[8,128,128]{2,1,0:T(8,128)S(1)}, u32[]{:S(2)}, u32[]{:S(2)}) collective-permute-start(f32[8,128,128]{2,1,0:T(8,128)S(1)} %collective-permute-done.10.v_ref), channel_id=1, source_target_pairs={{0,8},{8,16},{16,24},{1,9},{9,17},{17,25},{2,10},{10,18},{18,26},{... | collective-permute-start | bytes 1572872 | tf_op jit(solution)/shard_map/ppermute | solution.py:405
  73.7 16.9 %collective-permute-start.2 = (f32[512,128]{1,0:T(8,128)S(1)}, f32[512,128]{1,0:T(8,128)S(1)}, u32[]{:S(2)}, u32[]{:S(2)}) collective-permute-start(f32[512,128]{1,0:T(8,128)S(1)} %get-tuple-element.45), channel_id=1, source_target_pairs={{0,6},{1,7},{2,0},{3,1},{4,2},{5,3},{6,4},{7,5},{8,14},{9,15},{10,... | collective-permute-start | bytes 786440 | tf_op jit(solution)/shard_map/ppermute | solution.py:333
  77.3 18.7 %collective-permute-start.1 = (f32[512,128]{1,0:T(8,128)S(1)}, f32[512,128]{1,0:T(8,128)S(1)}, u32[]{:S(2)}, u32[]{:S(2)}) collective-permute-start(f32[512,128]{1,0:T(8,128)S(1)} %get-tuple-element.46), channel_id=1, source_target_pairs={{0,4},{1,5},{2,6},{3,7},{4,0},{5,1},{6,2},{7,3},{8,12},{9,13},{10,... | collective-permute-start | bytes 786440 | tf_op jit(solution)/shard_map/ppermute | solution.py:333
  80.6 15.4 %collective-permute-start = (f32[512,128]{1,0:T(8,128)S(1)}, f32[512,128]{1,0:T(8,128)S(1)}, u32[]{:S(2)}, u32[]{:S(2)}) collective-permute-start(f32[512,128]{1,0:T(8,128)S(1)} %get-tuple-element.47), channel_id=1, source_target_pairs={{0,2},{1,3},{2,4},{3,5},{4,6},{5,7},{6,0},{7,1},{8,10},{9,11},{10,... | collective-permute-start | bytes 786440 | tf_op jit(solution)/shard_map/ppermute | solution.py:333
  86.7 52.0 %collective-permute-start.13 = (f32[8,128,128]{2,1,0:T(8,128)}, f32[8,128,128]{2,1,0:T(8,128)S(1)}, u32[]{:S(2)}, u32[]{:S(2)}) collective-permute-start(f32[8,128,128]{2,1,0:T(8,128)} %shard_map.61), channel_id=1, source_target_pairs={{0,8},{8,16},{16,24},{1,9},{9,17},{17,25},{2,10},{10,18},{18,26},{... | collective-permute-start | bytes 1572872 | tf_op jit(solution)/shard_map/ppermute | solution.py:404
  88.7 26.7 %copy-start.10 = (f32[8,128,128]{2,1,0:T(8,128)}, f32[8,128,128]{2,1,0:T(8,128)S(1)}, u32[]{:S(2)}) copy-start(f32[8,128,128]{2,1,0:T(8,128)S(1)} %collective-permute-done.12.v_ref) | copy-start | bytes 1572868
  88.7 50.1 %collective-permute-start.14 = (f32[8,128,128]{2,1,0:T(8,128)S(1)}, f32[8,128,128]{2,1,0:T(8,128)S(1)}, u32[]{:S(2)}, u32[]{:S(2)}) collective-permute-start(f32[8,128,128]{2,1,0:T(8,128)S(1)} %collective-permute-done.12.v_ref), channel_id=1, source_target_pairs={{0,8},{8,16},{16,24},{1,9},{9,17},{17,25},{2,10},{10,18},{18,26},{... | collective-permute-start | bytes 1572872 | tf_op jit(solution)/shard_map/ppermute | solution.py:405
  90.6 5.4 %copy-start.13 = (f32[512,128]{1,0:T(8,128)}, f32[512,128]{1,0:T(8,128)S(1)}, u32[]{:S(2)}) copy-start(f32[512,128]{1,0:T(8,128)S(1)} %collective-permute-done.2.refs_3_) | copy-start | bytes 786436
  146.1 9.6 %collective-permute-start.17 = (f32[512,128]{1,0:T(8,128)S(1)}, f32[512,128]{1,0:T(8,128)S(1)}, u32[]{:S(2)}, u32[]{:S(2)}) collective-permute-start(f32[512,128]{1,0:T(8,128)S(1)} %get-tuple-element.41), channel_id=1, source_target_pairs={{0,6},{1,7},{2,0},{3,1},{4,2},{5,3},{6,4},{7,5},{8,14},{9,15},{10,... | collective-permute-start | bytes 786440 | tf_op jit(solution)/shard_map/ppermute | solution.py:333
  146.1 21.3 %collective-permute-start.16 = (f32[512,128]{1,0:T(8,128)S(1)}, f32[512,128]{1,0:T(8,128)S(1)}, u32[]{:S(2)}, u32[]{:S(2)}) collective-permute-start(f32[512,128]{1,0:T(8,128)S(1)} %get-tuple-element.42), channel_id=1, source_target_pairs={{0,4},{1,5},{2,6},{3,7},{4,0},{5,1},{6,2},{7,3},{8,12},{9,13},{10,... | collective-permute-start | bytes 786440 | tf_op jit(solution)/shard_map/ppermute | solution.py:333
  146.1 21.3 %collective-permute-start.15 = (f32[512,128]{1,0:T(8,128)S(1)}, f32[512,128]{1,0:T(8,128)S(1)}, u32[]{:S(2)}, u32[]{:S(2)}) collective-permute-start(f32[512,128]{1,0:T(8,128)S(1)} %get-tuple-element.43), channel_id=1, source_target_pairs={{0,2},{1,3},{2,4},{3,5},{4,6},{5,7},{6,0},{7,1},{8,10},{9,11},{10,... | collective-permute-start | bytes 786440 | tf_op jit(solution)/shard_map/ppermute | solution.py:333
  155.7 11.7 %copy-start.5 = (f32[512,128]{1,0:T(8,128)}, f32[512,128]{1,0:T(8,128)S(1)}, u32[]{:S(2)}) copy-start(f32[512,128]{1,0:T(8,128)S(1)} %collective-permute-done.17.refs_3_) | copy-start | bytes 786436
  (13 other events, 17.1 us)
